TPU v7x, 128 devices: a whole 4x4x4 slice. The times are simulated.
128 devices in a mesh: req: 8 (over y, core), tok: 16 (over x, z).
Axes of the slice: x: 4, y: 4, z: 4, core: 2. Of those that a mesh axis runs over, the one named last changes fastest.
Arguments:
- layer_input: bfloat16 [16384, 2048], P(('req', 'tok')), may hold values from -12 to 12
- q_in: bfloat16 [16384, 2048], P(('req', 'tok')), may hold values from -10 to 10
- k_in: bfloat16 [16384, 2048], P(('req', 'tok')), may hold values from -10 to 10
- v_in: bfloat16 [16384, 2048], P(('req', 'tok')), may hold values from -6 to 6
- segment_ids: int32 [8, 2048], P('req'), may hold values from 0 to 3, never falling along the last dimension, each value on 1 to 1024 neighbouring positions
- lambda_parts: float32 [4, 128], replicated, may hold values from -0.8 to 0.8
- out_weight: bfloat16 [2048, 2048], replicated, may hold values from -0.125 to 0.125
- ffn_gain: float32 [2048], replicated, may hold values from 0.1 to 1.9
- gate_weight: bfloat16 [2048, 5632], P(None, 'req'), may hold values from -0.125 to 0.125
- up_weight: bfloat16 [2048, 5632], P(None, 'req'), may hold values from -0.125 to 0.125
- down_weight: bfloat16 [5632, 2048], P('req'), may hold values from -0.078125 to 0.078125
- next_gain: float32 [2048], replicated, may hold values from 0.1 to 1.9
- qkv_weight: bfloat16 [2048, 6144], P(None, 'req'), may hold values from -0.125 to 0.125
- page_owner: int32 [8, 256], P('req'), may hold values from 0 to 15, as said below
- page_slot: int32 [8, 256], P('req'), may hold values from 0 to 15, as said below
Outputs:
- layer_output: bfloat16 [16384, 2048], P(('req', 'tok'))
- q_next: bfloat16 [16384, 2048], P(('req', 'tok'))
- page_cache: bfloat16 [2048, 8, 4096], P(('req', 'tok'))
Inputs may be any that keep to these rules, and one draw needn't show every extreme that they name: `segment_ids`: segment numbers never fall along a group; each of the 4 prompts of a group has 1 to 1024 tokens, one exactly 1024. `page_owner`: the 16 pages of each device name every device of its request group as owner exactly once. `page_slot`: within a request group every pair of owner and slot is named by exactly one page.
All inputs are finite; a program needn't handle non-finite values.
Results may differ from a plain program's by a relative error of at most 0.017.
Values may be sent and summed in bfloat16 or wider, within the bound.
A program may use at most 192 MiB of HBM per device.

v0:
```python
import math
import jax
import jax.numpy as jnp
from jax import lax
from jax.sharding import PartitionSpec as P

HEADS = 8
PAGE = 8
NEG_FILL = -1e30
LAMBDA_INIT = 0.2
EPSILON = 1e-05
MAX_SEG = 1024


def rms_rows(values):
    return values * lax.rsqrt(jnp.mean(values * values, axis=-1, keepdims=True) + EPSILON)


def lambda_value(lambda_parts):
    first_term = jnp.exp(jnp.sum(lambda_parts[0] * lambda_parts[1]))
    second_term = jnp.exp(jnp.sum(lambda_parts[2] * lambda_parts[3]))
    return first_term - second_term + LAMBDA_INIT


def body(
    layer_input,
    q_in,
    k_in,
    v_in,
    segment_ids,
    lambda_parts,
    out_weight,
    ffn_gain,
    gate_weight,
    up_weight,
    down_weight,
    next_gain,
    qkv_weight,
    page_owner,
    page_slot,
):
    row_count = q_in.shape[0]
    feat_width = q_in.shape[1]
    head_dim = feat_width // (2 * HEADS)
    peer_count = lax.axis_size("tok")
    tok_place = lax.axis_index("tok")
    seg_row = segment_ids[0]
    first_row = tok_place * row_count
    query_places = first_row + jnp.arange(row_count)
    query_segs = lax.dynamic_slice_in_dim(seg_row, first_row, row_count)
    lambda_mix = lambda_value(lambda_parts)
    score_scale = 1.0 / math.sqrt(head_dim)
    query_split = q_in.reshape(row_count, HEADS, 2, head_dim)
    run_max = jnp.full((HEADS, 2, row_count), NEG_FILL, jnp.float32)
    back = -(-(MAX_SEG - 1) // row_count)
    own_kv = jnp.concatenate([k_in, v_in], axis=1)
    all_kv = lax.all_gather(own_kv, "tok", axis=0, tiled=True)
    padded_kv = jnp.concatenate(
        [jnp.zeros((back * row_count, 2 * feat_width), all_kv.dtype), all_kv], axis=0
    )
    window = lax.dynamic_slice_in_dim(padded_kv, first_row, (back + 1) * row_count, 0)
    piece_len = window.shape[0]
    key_rows = window[:, :feat_width]
    value_rows = window[:, feat_width:]
    key_split = key_rows.reshape(piece_len, HEADS, 2, head_dim)
    value_split = value_rows.reshape(piece_len, HEADS, 2 * head_dim)
    key_places = (tok_place - back) * row_count + jnp.arange(piece_len)
    key_segs = jnp.take(seg_row, jnp.clip(key_places, 0, seg_row.shape[0] - 1))
    visible = (
        (key_places[None, :] >= 0)
        & (key_segs[None, :] == query_segs[:, None])
        & (key_places[None, :] <= query_places[:, None])
    )
    scores = (
        jnp.einsum("qhmd,khmd->hmqk", query_split, key_split, preferred_element_type=jnp.float32)
        * score_scale
    )
    scores = jnp.where(visible, scores, NEG_FILL)
    new_max = jnp.maximum(run_max, jnp.max(scores, axis=-1))
    weights = jnp.where(visible, jnp.exp(scores - new_max[..., None]), 0.0)
    totals = jnp.sum(weights, axis=-1)
    weighted = jnp.einsum(
        "hmqk,khe->hmqe",
        weights.astype(jnp.bfloat16),
        value_split,
        preferred_element_type=jnp.float32,
    )
    run_max, totals, weighted = (new_max, totals, weighted)
    map_outputs = weighted / totals[..., None]
    difference = map_outputs[:, 0] - lambda_mix * map_outputs[:, 1]
    head_outputs = rms_rows(difference) * (1.0 - LAMBDA_INIT)
    attention = (
        jnp.transpose(head_outputs, (1, 0, 2)).reshape(row_count, feat_width).astype(jnp.bfloat16)
    )
    residual_mid = (
        layer_input.astype(jnp.float32)
        + jnp.dot(attention, out_weight, preferred_element_type=jnp.float32)
    ).astype(jnp.bfloat16)
    gathered = lax.all_gather(residual_mid, "req", axis=0, tiled=True)
    normed = (rms_rows(gathered.astype(jnp.float32)) * ffn_gain).astype(jnp.bfloat16)
    gate_proj = jnp.dot(normed, gate_weight, preferred_element_type=jnp.float32)
    up_proj = jnp.dot(normed, up_weight, preferred_element_type=jnp.float32)
    hidden = (jax.nn.silu(gate_proj) * up_proj).astype(jnp.bfloat16)
    ffn_own = lax.psum_scatter(
        jnp.dot(hidden, down_weight, preferred_element_type=jnp.float32).astype(jnp.bfloat16),
        "req",
        scatter_dimension=0,
        tiled=True,
    ).astype(jnp.float32)
    layer_output = (residual_mid.astype(jnp.float32) + ffn_own).astype(jnp.bfloat16)
    next_normed = (rms_rows(layer_output.astype(jnp.float32)) * next_gain).astype(jnp.bfloat16)
    projected_cols = jnp.dot(
        lax.all_gather(next_normed, "req", axis=0, tiled=True),
        qkv_weight,
        preferred_element_type=jnp.float32,
    ).astype(jnp.bfloat16)
    projected = lax.all_to_all(projected_cols, "req", split_axis=0, concat_axis=1, tiled=True)
    q_next = projected[:, :feat_width]
    pages_dev = row_count // PAGE
    per_owner = pages_dev // peer_count
    key_values = projected[:, feat_width:].reshape(pages_dev, PAGE, 2 * feat_width)
    owner_all = page_owner[0].reshape(peer_count, pages_dev)
    slot_all = page_slot[0].reshape(peer_count, pages_dev)
    page_numbers = jnp.arange(pages_dev, dtype=jnp.int32)
    my_owners = lax.dynamic_index_in_dim(owner_all, tok_place, 0, keepdims=False)
    send_order = jnp.argsort(my_owners * pages_dev + page_numbers)
    outgoing = key_values[send_order].reshape(peer_count, per_owner, PAGE, 2 * feat_width)
    incoming = lax.all_to_all(outgoing, "tok", split_axis=0, concat_axis=0, tiled=True)
    rank_keys = jnp.where(
        owner_all == tok_place, page_numbers[None, :], pages_dev + page_numbers[None, :]
    )
    chosen_pages = jnp.argsort(rank_keys, axis=1)[:, :per_owner]
    slot_list = jnp.take_along_axis(slot_all, chosen_pages, axis=1).reshape(pages_dev)
    page_cache = (
        jnp.zeros((pages_dev, PAGE, 2 * feat_width), jnp.bfloat16)
        .at[slot_list]
        .set(incoming.reshape(pages_dev, PAGE, 2 * feat_width))
    )
    return (layer_output, q_next, page_cache)


def solution(mesh):
    in_specs = (
        P(("req", "tok"), None),
        P(("req", "tok"), None),
        P(("req", "tok"), None),
        P(("req", "tok"), None),
        P("req", None),
        P(),
        P(),
        P(),
        P(None, "req"),
        P(None, "req"),
        P("req", None),
        P(),
        P(None, "req"),
        P("req", None),
        P("req", None),
    )
    out_specs = (P(("req", "tok"), None), P(("req", "tok"), None), P(("req", "tok"), None, None))
    return jax.shard_map(body, mesh=mesh, in_specs=in_specs, out_specs=out_specs, check_vma=False)
```

profile of v0, /device:TPU:0, one launch (start us, length us, event | category | flops | bytes accessed | tf_op | source)
XLA Modules:
  0.0 369.7 jit_solution(3113207393178205079)
XLA Ops:
  7.2 2.2 copy.38
  9.4 2.0 copy.39
  11.5 2.2 pad_maximum_fusion
  13.8 2.2 reshape.141
  18.0 6.5 %gather_fusion = s32[1152]{0:T(1024)S(1)} fusion(s32[2048]{0:T(1024)S(1)} %bitcast.64, s32[2048]{0:T(1024)S(1)} %pad_clamp_fusion), kind=kCustom, calls=%fused_computation | custom fusion | bytes 13824 | tf_op jit(solution)/shard_map/jit(_take)/gather | solution.py:68
  25.6 112.0 %all-gather.4.cloned.1.call-done = bf16[2048,4096]{0,1:T(8,128)(2,1)} async-done(((bf16[128,4096]{0,1:T(8,128)(2,1)}), bf16[2048,4096]{0,1:T(8,128)(2,1)}) %all-gather.4.cloned.1.call-update) | async-done | bytes 16777232 | tf_op jit(solution)/shard_map/all_gather | solution.py:57
  137.5 5.1 %pad_dynamic-slice_fusion.1 = (bf16[1152,2048]{0,1:T(8,128)(2,1)}, bf16[1152,2048]{0,1:T(8,128)(2,1)S(1)}) fusion(s32[]{:T(128)S(6)} %select_n.70, s32[]{:T(128)S(6)} %add.181, bf16[2048,4096]{0,1:T(8,128)(2,1)} %all-gather.4.cloned.1.call-done), kind=kLoop, calls=%fused_computation.5 | loop fusion | bytes 26214408 | tf_op jit(solution)/shard_map/slice | solution.py:64
  142.6 2.5 fusion.3
  145.1 2.3 fusion.4
  147.4 1.3 copy-done.2
  148.7 8.3 %broadcast_divide_fusion = f32[8,2,128,256]{3,2,1,0:T(8,128)S(1)} fusion(f32[8,2,128]{2,1,0:T(2,128)S(1)} %fusion.4, bf16[1152,8,256,1]{0,2,3,1:T(8,128)(2,1)} %bitcast.68, f32[8,2,1152,128]{3,2,1,0:T(8,128)} %copy-done.2, f32[8,2,128]{2,1,0:T(2,128)S(1)} %broadcast_maximum_fusion, pred[128,1152]{0,1:T(8,128)(4,1)S(1)} %compare_and_fusion), kind=kOutput, calls=%fused_computation.41 | convolution fusion | flops 1220280320 | bytes 16416768 | tf_op jit(solution)/shard_map/hmqk,khe->hmqe/dot_general | solution.py:82
  157.2 1.1 fusion.26
  158.3 2.0 copy.44
  160.3 5.7 %fusion.13 = bf16[128,2048]{1,0:T(8,128)(2,1)} fusion(bf16[128,2048]{0,1:T(8,128)(2,1)} %bitcast.70, bf16[2048,2048]{1,0:T(8,128)(2,1)} %param.21, bf16[128,2048]{1,0:T(8,128)(2,1)} %param.15), kind=kOutput, calls=%fused_computation.25 | convolution fusion | flops 1074528256 | bytes 9961472 | tf_op jit(solution)/shard_map/dot_general | solution.py:97
  166.3 33.9 %all-gather.6.cloned.1.call-done = bf16[1024,2048]{1,0:T(8,128)(2,1)} async-done(((bf16[128,2048]{1,0:T(8,128)(2,1)}), bf16[1024,2048]{1,0:T(8,128)(2,1)}) %all-gather.6.cloned.1.call-update) | async-done | bytes 4194320 | tf_op jit(solution)/shard_map/all_gather | solution.py:99
  200.1 3.2 fusion
  203.6 6.7 %fusion.15 = f32[1024,704]{0,1:T(8,128)} fusion(bf16[2048,704]{0,1:T(8,128)(2,1)} %param.23, bf16[1024,2048]{1,0:T(8,128)(2,1)S(1)} %copy-done.4, f32[2048]{0:T(1024)S(1)} %copy-done.11, f32[1024]{0:T(1024)S(1)} %add_rsqrt_fusion), kind=kOutput, calls=%fused_computation.29 | convolution fusion | flops 2961178624 | bytes 9973760 | tf_op jit(solution)/shard_map/dot_general | solution.py:101
  210.3 12.4 %convolution_convert_fusion = bf16[1024,2048]{1,0:T(8,128)(2,1)} fusion(bf16[704,2048]{1,0:T(8,128)(2,1)} %param.25, f32[1024,704]{0,1:T(8,128)} %fusion.15, bf16[2048,704]{0,1:T(8,128)(2,1)} %param.24, bf16[1024,2048]{1,0:T(8,128)(2,1)} %all-gather.6.cloned.1.call-done, f32[2048]{0:T(1024)S(1)} %copy-done.11, f32[1024]{0:T(1024)S(1)} %add_rsqrt_fusion), kind=kOutput, calls=%fused_computation.22 | convolution fusion | flops 5920391168 | bytes 17051648 | tf_op jit(solution)/shard_map/dot_general | solution.py:105
  222.8 37.9 %reduce-scatter.2.cloned.1.call-done = bf16[128,2048]{1,0:T(8,128)(2,1)} async-done(((bf16[1024,2048]{1,0:T(8,128)(2,1)}), bf16[128,2048]{1,0:T(8,128)(2,1)}) %reduce-scatter.2.cloned.1.call-update) | async-done | bytes 524304 | tf_op jit(solution)/shard_map/reduce_scatter | solution.py:104
  260.6 1.5 fusion.19
  263.9 31.2 %all-gather.8.cloned.1.call-done = bf16[1024,2048]{1,0:T(8,128)(2,1)} async-done(((bf16[128,2048]{1,0:T(8,128)(2,1)}), bf16[1024,2048]{1,0:T(8,128)(2,1)}) %all-gather.8.cloned.1.call-update) | async-done | bytes 4194320 | tf_op jit(solution)/shard_map/all_gather | solution.py:113
  295.1 6.8 %convolution_convert_fusion.1 = bf16[1024,768]{1,0:T(8,128)(2,1)} fusion(bf16[1024,2048]{1,0:T(8,128)(2,1)} %all-gather.8.cloned.1.call-done, bf16[2048,768]{1,0:T(8,128)(2,1)S(1)} %copy-done), kind=kOutput, calls=%fused_computation.26 | convolution fusion | flops 3222011904 | bytes 8912896 | tf_op jit(solution)/shard_map/dot_general | solution.py:112
  301.8 4.3 %all-to-all-start = ((bf16[8,128,768]{2,1,0:T(8,128)(2,1)}), bf16[8,128,768]{2,1,0:T(8,128)(2,1)}, u32[]{:S(2)}, u32[]{:S(2)}) async-start(bf16[8,128,768]{2,1,0:T(8,128)(2,1)} %bitcast.71), calls=%async_computation.1 | async-start | bytes 3145728 | tf_op jit(solution)/shard_map/all_to_all | solution.py:117
  308.2 1.2 sort.35
  309.5 18.2 %all-to-all-done = bf16[8,128,768]{2,1,0:T(8,128)(2,1)} async-done(((bf16[8,128,768]{2,1,0:T(8,128)(2,1)}), bf16[8,128,768]{2,1,0:T(8,128)(2,1)}, u32[]{:S(2)}, u32[]{:S(2)}) %all-to-all-start) | async-done | bytes 1572896 | tf_op jit(solution)/shard_map/all_to_all | solution.py:117
  327.7 1.6 copy.52
  329.3 1.1 copy-done.3
  331.5 2.8 gather_fusion.1
  334.3 7.0 %all-to-all-start.1 = ((bf16[16,1,8,4096]{3,2,1,0:T(8,128)(2,1)}), bf16[16,1,8,4096]{3,2,1,0:T(8,128)(2,1)}, u32[]{:S(2)}, u32[]{:S(2)}) async-start(bf16[16,1,8,4096]{3,2,1,0:T(8,128)(2,1)} %bitcast.69), calls=%async_computation.2 | async-start | bytes 2097152 | tf_op jit(solution)/shard_map/all_to_all | solution.py:128
  342.8 1.9 slice.52
  344.7 14.1 %all-to-all-done.1 = bf16[16,1,8,4096]{3,2,1,0:T(8,128)(2,1)} async-done(((bf16[16,1,8,4096]{3,2,1,0:T(8,128)(2,1)}), bf16[16,1,8,4096]{3,2,1,0:T(8,128)(2,1)}, u32[]{:S(2)}, u32[]{:S(2)}) %all-to-all-start.1) | async-done | bytes 1048608 | tf_op jit(solution)/shard_map/all_to_all | solution.py:128
  359.8 3.4 scatter_fusion
  (66 shorter events, 10.1 us)
Async XLA Ops:
  7.2 287.9 %copy-start = (bf16[2048,768]{1,0:T(8,128)(2,1)S(1)}, bf16[2048,768]{1,0:T(8,128)(2,1)}, u32[]{:S(2)}) copy-start(bf16[2048,768]{1,0:T(8,128)(2,1)} %param.27) | copy-start | bytes 9437188
  7.2 8.8 %copy-start.8 = (f32[4,128]{1,0:T(4,128)S(1)}, f32[4,128]{1,0:T(4,128)}, u32[]{:S(2)}) copy-start(f32[4,128]{1,0:T(4,128)} %param.20) | copy-start | bytes 6148
  7.2 10.8 %copy-start.1 = (s32[1,2048]{1,0:T(1,128)S(1)}, s32[1,2048]{1,0:T(1,128)}, u32[]{:S(2)}) copy-start(s32[1,2048]{1,0:T(1,128)} %param.19) | copy-start | bytes 24580
  7.2 130.3 %all-gather.4.cloned.1.call-start = ((), (), s32[]{:S(2)}) async-start(), calls=%async_computation.3 | async-start | bytes 17825792 | tf_op jit(solution)/shard_map/all_gather | solution.py:57
  13.7 186.4 %all-gather.6.cloned.1.call-start = ((), (), s32[]{:S(2)}) async-start(), calls=%async_computation.4 | async-start | bytes 4718592 | tf_op jit(solution)/shard_map/all_gather | solution.py:99
  137.5 5.1 %copy-start.5 = (bf16[128,8,2,128]{3,2,1,0:T(2,128)(2,1)S(1)}, bf16[128,8,2,128]{3,2,1,0:T(2,128)(2,1)}, u32[]{:S(2)}) copy-start(bf16[128,8,2,128]{3,2,1,0:T(2,128)(2,1)} %reshape.141) | copy-start | bytes 1572868
  145.1 3.6 copy-start.2
  166.0 37.4 %copy-start.11 = (f32[2048]{0:T(1024)S(1)}, f32[2048]{0:T(1024)}, u32[]{:S(2)}) copy-start(f32[2048]{0:T(1024)} %param.22) | copy-start | bytes 24580
  166.0 94.6 %reduce-scatter.2.cloned.1.call-start = ((), (), s32[]{:S(2)}) async-start(), calls=%async_computation.5 | async-start | bytes 4718592 | tf_op jit(solution)/shard_map/reduce_scatter | solution.py:104
  200.1 3.4 copy-start.4
  222.7 40.2 %copy-start.7 = (f32[2048]{0:T(1024)S(1)}, f32[2048]{0:T(1024)}, u32[]{:S(2)}) copy-start(f32[2048]{0:T(1024)} %param.26) | copy-start | bytes 24580
  222.7 72.4 %all-gather.8.cloned.1.call-start = ((), (), s32[]{:S(2)}) async-start(), calls=%async_computation.6 | async-start | bytes 4718592 | tf_op jit(solution)/shard_map/all_gather | solution.py:113
  262.1 0.8 copy-start.6
  263.9 42.8 %copy-start.9 = (s32[1,256]{1,0:T(1,128)S(1)}, s32[1,256]{1,0:T(1,128)}, u32[]{:S(2)}) copy-start(s32[1,256]{1,0:T(1,128)} %param.28) | copy-start | bytes 3076
  263.9 43.6 %copy-start.10 = (s32[1,256]{1,0:T(1,128)S(1)}, s32[1,256]{1,0:T(1,128)}, u32[]{:S(2)}) copy-start(s32[1,256]{1,0:T(1,128)} %param.29) | copy-start | bytes 3076
  301.8 25.9 %all-to-all-start = ((bf16[8,128,768]{2,1,0:T(8,128)(2,1)}), bf16[8,128,768]{2,1,0:T(8,128)(2,1)}, u32[]{:S(2)}, u32[]{:S(2)}) async-start(bf16[8,128,768]{2,1,0:T(8,128)(2,1)} %bitcast.71), calls=%async_computation.1 | async-start | bytes 3145728 | tf_op jit(solution)/shard_map/all_to_all | solution.py:117
  329.3 1.2 copy-start.3
  334.3 24.4 %all-to-all-start.1 = ((bf16[16,1,8,4096]{3,2,1,0:T(8,128)(2,1)}), bf16[16,1,8,4096]{3,2,1,0:T(8,128)(2,1)}, u32[]{:S(2)}, u32[]{:S(2)}) async-start(bf16[16,1,8,4096]{3,2,1,0:T(8,128)(2,1)} %bitcast.69), calls=%async_computation.2 | async-start | bytes 2097152 | tf_op jit(solution)/shard_map/all_to_all | solution.py:128
Sparse Core Ops, SparseCore 0:
  13.9 123.6 all-gather.3
  166.1 33.9 all-gather.5
  222.8 37.7 reduce-scatter.1
  264.0 31.0 all-gather.7
where the time goes:
time: 370 us
  waiting for transfers between devices  247 us (67%)
  matrix products  42.3 us (11%)
  local copies, waits for them, and re-layouts  36.7 us (10%)
  other arithmetic  16.7 us (5%)
  between operations  15.3 us (4%)
  starting transfers between devices  11.6 us (3%)
    all_gather x1, waiting for transfers between devices, body(): all_kv = lax.all_gather(own_kv, 'tok', axis=0, tiled=True)  112 us
    reduce_scatter x1, waiting for transfers between devices, body(): lax.psum_scatter(jnp.dot(hidden, down_weight, preferred_element_type=jnp....  37.9 us
    all_gather x1, waiting for transfers between devices, body(): gathered = lax.all_gather(residual_mid, 'req', axis=0, tiled=True)  33.9 us
    all_gather x1, waiting for transfers between devices, body(): lax.all_gather(next_normed, 'req', axis=0, tiled=True)  31.2 us
    all_to_all x1, waiting for transfers between devices, body(): lax.all_to_all(projected_cols, 'req', split_axis=0, concat_axis=1, tiled=...  18.2 us
    all_to_all x1, waiting for transfers between devices, body(): lax.all_to_all(outgoing, 'tok', split_axis=0, concat_axis=0, tiled=True)  14.1 us
    dot_general x1, matrix products, body(): jnp.dot(hidden, down_weight, preferred_element_type=jnp.float32)  12.4 us
    dot_general x1, matrix products, body(): jnp.einsum('hmqk,khe->hmqe', weights.astype(jnp.bfloat16), value_split, p...  8.27 us
  transfers between devices with their start and end apart: 6, of which 6 were waited for; matrix products, arithmetic and copies ran while one was open for 5% of the time, Pallas kernels for 0%

commit v1 on v0

--- a/solution.py
+++ b/solution.py
@@ -10,6 +10,15 @@
 LAMBDA_INIT = 0.2
 EPSILON = 1e-05
 MAX_SEG = 1024
+edges_wait = lambda local_block, a_name: jnp.concatenate(
+    jax.lax.all_to_all(
+        jnp.stack([local_block for _ in range(jax.lax.axis_size(a_name))]),
+        axis_name=a_name,
+        split_axis=0,
+        concat_axis=0,
+    ),
+    0,
+)
 
 
 def rms_rows(values):
@@ -96,7 +105,7 @@
         layer_input.astype(jnp.float32)
         + jnp.dot(attention, out_weight, preferred_element_type=jnp.float32)
     ).astype(jnp.bfloat16)
-    gathered = lax.all_gather(residual_mid, "req", axis=0, tiled=True)
+    gathered = edges_wait(residual_mid, "req")
     normed = (rms_rows(gathered.astype(jnp.float32)) * ffn_gain).astype(jnp.bfloat16)
     gate_proj = jnp.dot(normed, gate_weight, preferred_element_type=jnp.float32)
     up_proj = jnp.dot(normed, up_weight, preferred_element_type=jnp.float32)

time: 370 us -> 389 us (1.051)
  blocking collectives: 0 us -> 54.4 us
  waiting for transfers between devices: 247 us -> 213 us
    all_to_all x0 -> x1, blocking collectives: none -> 54.4 us  [jax.lax.all_to_all(jnp.stack([local_block for _ in range(jax.lax.axis_siz...]
    all_gather x1 -> x0, waiting for transfers between devices: 33.9 us -> none  [body(): gathered = lax.all_gather(residual_mid, 'req', axis=0, tiled=True)]
    unnamed x28 -> x32, local copies, waits for them, and re-layouts: 8.25 us -> 10 us
  transfers between devices with their start and end apart: 6 -> 5, of which waited for: 6 -> 5; matrix products, arithmetic and copies ran while one was open for 5% -> 4% of each run, Pallas kernels for 0% -> 0%
where the time goes in v1:
time: 389 us; the launch traced here: 388 us
  waiting for transfers between devices  213 us (55%)
  blocking collectives  54.4 us (14%)
  matrix products  39.1 us (10%)
  local copies, waits for them, and re-layouts  39 us (10%)
  other arithmetic  15.3 us (4%)
  between operations  15.3 us (4%)
  starting transfers between devices  11.4 us (3%)
    all_gather x1, waiting for transfers between devices, body(): all_kv = lax.all_gather(own_kv, 'tok', axis=0, tiled=True)  112 us
    all_to_all x1, blocking collectives, jax.lax.all_to_all(jnp.stack([local_block for _ in range(jax.lax.axis_siz...  54.4 us
    reduce_scatter x1, waiting for transfers between devices, body(): lax.psum_scatter(jnp.dot(hidden, down_weight, preferred_element_type=jnp....  38 us
    all_gather x1, waiting for transfers between devices, body(): lax.all_gather(next_normed, 'req', axis=0, tiled=True)  31 us
    all_to_all x1, waiting for transfers between devices, body(): lax.all_to_all(projected_cols, 'req', split_axis=0, concat_axis=1, tiled=...  18.2 us
    all_to_all x1, waiting for transfers between devices, body(): lax.all_to_all(outgoing, 'tok', split_axis=0, concat_axis=0, tiled=True)  14.1 us
    dot_general x1, matrix products, body(): jnp.dot(hidden, down_weight, preferred_element_type=jnp.float32)  12 us
    unnamed x32, local copies, waits for them, and re-layouts  10 us
  transfers between devices with their start and end apart: 5, of which 5 were waited for; matrix products, arithmetic and copies ran while one was open for 4% of the time, Pallas kernels for 0%

profile of v1, /device:TPU:0, one launch (start us, length us, event | category | flops | bytes accessed | tf_op | source)
XLA Modules:
  0.0 387.9 jit_solution(7122246752290326810)
XLA Ops:
  7.2 2.2 copy.47
  9.4 2.0 copy.48
  11.5 2.2 pad_maximum_fusion
  13.8 2.2 reshape.155
  18.0 6.5 %gather_fusion = s32[1152]{0:T(1024)S(1)} fusion(s32[2048]{0:T(1024)S(1)} %bitcast.74, s32[2048]{0:T(1024)S(1)} %pad_clamp_fusion), kind=kCustom, calls=%fused_computation | custom fusion | bytes 13824 | tf_op jit(solution)/shard_map/jit(_take)/gather | solution.py:77
  25.6 112.0 %all-gather.3.cloned.1.call-done = bf16[2048,4096]{0,1:T(8,128)(2,1)} async-done(((bf16[128,4096]{0,1:T(8,128)(2,1)}), bf16[2048,4096]{0,1:T(8,128)(2,1)}) %all-gather.3.cloned.1.call-update) | async-done | bytes 16777232 | tf_op jit(solution)/shard_map/all_gather | solution.py:66
  137.5 5.1 %pad_dynamic-slice_fusion.1 = (bf16[1152,2048]{0,1:T(8,128)(2,1)}, bf16[1152,2048]{0,1:T(8,128)(2,1)S(1)}) fusion(s32[]{:T(128)S(6)} %select_n.70, s32[]{:T(128)S(6)} %add.179, bf16[2048,4096]{0,1:T(8,128)(2,1)} %all-gather.3.cloned.1.call-done), kind=kLoop, calls=%fused_computation.5 | loop fusion | bytes 26214408 | tf_op jit(solution)/shard_map/slice | solution.py:73
  142.6 2.5 fusion.2
  145.1 2.3 fusion.3
  147.4 1.3 copy-done.2
  148.7 8.3 %broadcast_divide_fusion = f32[8,2,128,256]{3,2,1,0:T(8,128)S(1)} fusion(f32[8,2,128]{2,1,0:T(2,128)S(1)} %fusion.3, bf16[1152,8,256,1]{0,2,3,1:T(8,128)(2,1)} %bitcast.78, f32[8,2,1152,128]{3,2,1,0:T(8,128)} %copy-done.2, f32[8,2,128]{2,1,0:T(2,128)S(1)} %broadcast_maximum_fusion, pred[128,1152]{0,1:T(8,128)(4,1)S(1)} %compare_and_fusion), kind=kOutput, calls=%fused_computation.39 | convolution fusion | flops 1220280320 | bytes 16416768 | tf_op jit(solution)/shard_map/hmqk,khe->hmqe/dot_general | solution.py:91
  157.2 1.1 fusion.20
  158.3 2.0 copy.53
  160.3 4.9 %fusion.12 = bf16[128,2048]{1,0:T(8,128)(2,1)S(1)} fusion(bf16[128,2048]{0,1:T(8,128)(2,1)} %bitcast.80, bf16[2048,2048]{1,0:T(8,128)(2,1)} %param.21, bf16[128,2048]{1,0:T(8,128)(2,1)} %param.15), kind=kOutput, calls=%fused_computation.24 | convolution fusion | flops 1074528256 | bytes 9961472 | tf_op jit(solution)/shard_map/dot_general | solution.py:106
  165.7 54.4 %all_to_all.29 = bf16[8,128,2048]{2,1,0:T(8,128)(2,1)S(1)} all-to-all(bf16[8,128,2048]{2,1,0:T(8,128)(2,1)S(1)} %stack.2), channel_id=1, replica_groups=mesh['req'=8,'tok'=16] {'req'}, dimensions={0} | all-to-all | bytes 8388608 | tf_op jit(solution)/shard_map/all_to_all | solution.py:14
  222.1 2.0 copy-done.5
  224.1 4.8 %fusion.35 = f32[1024,704]{0,1:T(8,128)} fusion(bf16[1024,2048]{1,0:T(8,128)(2,1)S(1)} %fusion.1, bf16[2048,704]{0,1:T(8,128)(2,1)S(1)} %copy-done.13), kind=kOutput, calls=%fused_computation.79 | convolution fusion | flops 2952790016 | bytes 9961472 | tf_op jit(solution)/shard_map/dot_general | solution.py:110
  228.9 12.0 %convolution_convert_fusion = bf16[1024,2048]{1,0:T(8,128)(2,1)} fusion(bf16[704,2048]{1,0:T(8,128)(2,1)} %param.25, f32[1024,704]{0,1:T(8,128)} %fusion.35, bf16[1024,2048]{1,0:T(8,128)(2,1)} %copy-done.5, bf16[2048,704]{0,1:T(8,128)(2,1)} %param.24), kind=kOutput, calls=%fused_computation.21 | convolution fusion | flops 5912002560 | bytes 17039360 | tf_op jit(solution)/shard_map/dot_general | solution.py:114
  241.0 38.0 %reduce-scatter.2.cloned.1.call-done = bf16[128,2048]{1,0:T(8,128)(2,1)} async-done(((bf16[1024,2048]{1,0:T(8,128)(2,1)}), bf16[128,2048]{1,0:T(8,128)(2,1)}) %reduce-scatter.2.cloned.1.call-update) | async-done | bytes 524304 | tf_op jit(solution)/shard_map/reduce_scatter | solution.py:113
  279.0 1.5 fusion.13
  282.2 31.0 %all-gather.5.cloned.1.call-done = bf16[1024,2048]{1,0:T(8,128)(2,1)} async-done(((bf16[128,2048]{1,0:T(8,128)(2,1)}), bf16[1024,2048]{1,0:T(8,128)(2,1)}) %all-gather.5.cloned.1.call-update) | async-done | bytes 4194320 | tf_op jit(solution)/shard_map/all_gather | solution.py:122
  313.3 6.8 %convolution_convert_fusion.1 = bf16[1024,768]{1,0:T(8,128)(2,1)} fusion(bf16[1024,2048]{1,0:T(8,128)(2,1)} %all-gather.5.cloned.1.call-done, bf16[2048,768]{1,0:T(8,128)(2,1)S(1)} %copy-done), kind=kOutput, calls=%fused_computation.25 | convolution fusion | flops 3222011904 | bytes 8912896 | tf_op jit(solution)/shard_map/dot_general | solution.py:121
  320.0 4.3 %all-to-all-start.1 = ((bf16[8,128,768]{2,1,0:T(8,128)(2,1)}), bf16[8,128,768]{2,1,0:T(8,128)(2,1)}, u32[]{:S(2)}, u32[]{:S(2)}) async-start(bf16[8,128,768]{2,1,0:T(8,128)(2,1)} %bitcast.81), calls=%async_computation.2 | async-start | bytes 3145728 | tf_op jit(solution)/shard_map/all_to_all | solution.py:126
  326.4 1.2 sort.35
  327.7 18.2 %all-to-all-done.1 = bf16[8,128,768]{2,1,0:T(8,128)(2,1)} async-done(((bf16[8,128,768]{2,1,0:T(8,128)(2,1)}), bf16[8,128,768]{2,1,0:T(8,128)(2,1)}, u32[]{:S(2)}, u32[]{:S(2)}) %all-to-all-start.1) | async-done | bytes 1572896 | tf_op jit(solution)/shard_map/all_to_all | solution.py:126
  345.9 1.6 copy.61
  347.5 1.1 copy-done.3
  349.7 2.8 gather_fusion.1
  352.5 7.0 %all-to-all-start.2 = ((bf16[16,1,8,4096]{3,2,1,0:T(8,128)(2,1)}), bf16[16,1,8,4096]{3,2,1,0:T(8,128)(2,1)}, u32[]{:S(2)}, u32[]{:S(2)}) async-start(bf16[16,1,8,4096]{3,2,1,0:T(8,128)(2,1)} %bitcast.79), calls=%async_computation.3 | async-start | bytes 2097152 | tf_op jit(solution)/shard_map/all_to_all | solution.py:137
  361.0 1.9 slice.52
  362.9 14.1 %all-to-all-done.2 = bf16[16,1,8,4096]{3,2,1,0:T(8,128)(2,1)} async-done(((bf16[16,1,8,4096]{3,2,1,0:T(8,128)(2,1)}), bf16[16,1,8,4096]{3,2,1,0:T(8,128)(2,1)}, u32[]{:S(2)}, u32[]{:S(2)}) %all-to-all-start.2) | async-done | bytes 1048608 | tf_op jit(solution)/shard_map/all_to_all | solution.py:137
  378.0 3.4 scatter_fusion
  (70 shorter events, 12.1 us)
Async XLA Ops:
  7.2 306.1 %copy-start = (bf16[2048,768]{1,0:T(8,128)(2,1)S(1)}, bf16[2048,768]{1,0:T(8,128)(2,1)}, u32[]{:S(2)}) copy-start(bf16[2048,768]{1,0:T(8,128)(2,1)} %param.27) | copy-start | bytes 9437188
  7.2 8.8 %copy-start.10 = (f32[4,128]{1,0:T(4,128)S(1)}, f32[4,128]{1,0:T(4,128)}, u32[]{:S(2)}) copy-start(f32[4,128]{1,0:T(4,128)} %param.20) | copy-start | bytes 6148
  7.2 10.8 %copy-start.1 = (s32[1,2048]{1,0:T(1,128)S(1)}, s32[1,2048]{1,0:T(1,128)}, u32[]{:S(2)}) copy-start(s32[1,2048]{1,0:T(1,128)} %param.19) | copy-start | bytes 24580
  7.2 130.3 %all-gather.3.cloned.1.call-start = ((), (), s32[]{:S(2)}) async-start(), calls=%async_computation.4 | async-start | bytes 17825792 | tf_op jit(solution)/shard_map/all_gather | solution.py:66
  13.7 265.2 %reduce-scatter.2.cloned.1.call-start = ((), (), s32[]{:S(2)}) async-start(), calls=%async_computation.5 | async-start | bytes 4718592 | tf_op jit(solution)/shard_map/reduce_scatter | solution.py:113
  137.5 5.1 %copy-start.6 = (bf16[128,8,2,128]{3,2,1,0:T(2,128)(2,1)S(1)}, bf16[128,8,2,128]{3,2,1,0:T(2,128)(2,1)}, u32[]{:S(2)}) copy-start(bf16[128,8,2,128]{3,2,1,0:T(2,128)(2,1)} %reshape.155) | copy-start | bytes 1572868
  145.1 3.6 copy-start.2
  165.2 55.0 %copy-start.4 = (bf16[128,2048]{1,0:T(8,128)(2,1)}, bf16[128,2048]{1,0:T(8,128)(2,1)S(1)}, u32[]{:S(2)}) copy-start(bf16[128,2048]{1,0:T(8,128)(2,1)S(1)} %fusion.12) | copy-start | bytes 1572868
  220.2 0.9 copy-start.8
  221.1 3.0 copy-start.13
  222.1 2.0 copy-start.5
  240.9 40.3 %copy-start.9 = (f32[2048]{0:T(1024)S(1)}, f32[2048]{0:T(1024)}, u32[]{:S(2)}) copy-start(f32[2048]{0:T(1024)} %param.26) | copy-start | bytes 24580
  240.9 72.3 %all-gather.5.cloned.1.call-start = ((), (), s32[]{:S(2)}) async-start(), calls=%async_computation.6 | async-start | bytes 4718592 | tf_op jit(solution)/shard_map/all_gather | solution.py:122
  280.4 0.8 copy-start.7
  282.2 42.6 %copy-start.11 = (s32[1,256]{1,0:T(1,128)S(1)}, s32[1,256]{1,0:T(1,128)}, u32[]{:S(2)}) copy-start(s32[1,256]{1,0:T(1,128)} %param.28) | copy-start | bytes 3076
  282.2 43.4 %copy-start.12 = (s32[1,256]{1,0:T(1,128)S(1)}, s32[1,256]{1,0:T(1,128)}, u32[]{:S(2)}) copy-start(s32[1,256]{1,0:T(1,128)} %param.29) | copy-start | bytes 3076
  320.0 25.9 %all-to-all-start.1 = ((bf16[8,128,768]{2,1,0:T(8,128)(2,1)}), bf16[8,128,768]{2,1,0:T(8,128)(2,1)}, u32[]{:S(2)}, u32[]{:S(2)}) async-start(bf16[8,128,768]{2,1,0:T(8,128)(2,1)} %bitcast.81), calls=%async_computation.2 | async-start | bytes 3145728 | tf_op jit(solution)/shard_map/all_to_all | solution.py:126
  347.5 1.2 copy-start.3
  352.5 24.5 %all-to-all-start.2 = ((bf16[16,1,8,4096]{3,2,1,0:T(8,128)(2,1)}), bf16[16,1,8,4096]{3,2,1,0:T(8,128)(2,1)}, u32[]{:S(2)}, u32[]{:S(2)}) async-start(bf16[16,1,8,4096]{3,2,1,0:T(8,128)(2,1)} %bitcast.79), calls=%async_computation.3 | async-start | bytes 2097152 | tf_op jit(solution)/shard_map/all_to_all | solution.py:137
Sparse Core Ops, SparseCore 0:
  13.9 123.6 all-gather.2
  241.0 37.8 reduce-scatter.1
  282.3 30.8 all-gather.4
